TPU v7x, 256 devices: a whole 4x4x8 slice. The times are simulated.
256 devices in a mesh: row: 16 (over y_hi, x, core), col: 16 (over z, y_lo).
Axes of the slice: x: 4, y: 4 (y_hi: 2, y_lo: 2; y = y_hi * 2 + y_lo), z: 8, core: 2. Of those that a mesh axis runs over, the one named last changes fastest.
Arguments:
- hessenberg: float32 [16384, 16384], P('row', 'col'), may hold values from -6 to 6, as said below
- factors: float32 [3, 32, 512, 512], P(None, 'row', 'col'), may hold values from -1 to 1, as said below
- active: int32 [3, 32], replicated, may hold values 0 or 1
Outputs:
- updated_slab: float32 [16384, 16384], P('row', 'col')
Inputs may be any that keep to these rules, and one draw needn't show every extreme that they name: `hessenberg`: in global order, zero below the first subdiagonal. Each factors[f, s] is orthogonal up to float32 rounding.
All inputs are finite; a program needn't handle non-finite values.
Results may differ from a plain program's by a relative error of at most 0.0001.
Values sent between devices are 32-bit elements; how exact they have to be, the bound alone decides.
A program may use at most 64 MiB of HBM per device.

v0:
```python
import jax
import jax.numpy as jnp
from jax import lax
from jax.sharding import PartitionSpec as P

PRECISE = lax.Precision.HIGHEST


def passed_along(value, axis, steps):
    count = lax.axis_size(axis)
    pairs = [(source, (source + steps) % count) for source in range(count)]
    return lax.ppermute(value, axis, pairs)


def left_apply(factor, stacked):
    return jnp.einsum("kab,kan->kbn", factor, stacked, precision=PRECISE)


def right_apply(stacked, factor):
    return jnp.einsum("nka,kab->nkb", stacked, factor, precision=PRECISE)


def effective(factor, flag_row):
    identity = jnp.eye(factor.shape[-1], dtype=jnp.float32)
    return jnp.where(flag_row[:, None, None] > 0, factor, identity)


def wrap_fix(received, at_edge, offset_by, along_dim):
    return jnp.where(at_edge, jnp.roll(received, offset_by, axis=along_dim), received)


def sort_columns(collected, grid_rows):
    phases, all_blocks, pieces, window = collected.shape
    natural = collected.reshape(
        phases, grid_rows, all_blocks // grid_rows, pieces, window
    ).transpose(0, 2, 1, 3, 4)
    return natural.transpose(0, 2, 1, 3, 4)


def local(hessenberg, factors, active):
    rows_here, cols_here = hessenberg.shape
    window = factors.shape[-1]
    half_win = window // 2
    phases = factors.shape[0]
    grid_rows = lax.axis_size("row")
    grid_cols = lax.axis_size("col")
    row_index = lax.axis_index("row")
    col_index = lax.axis_index("col")
    row_blocks = rows_here // window
    col_blocks = cols_here // window
    all_blocks = row_blocks * grid_rows
    slot_row = jnp.arange(row_blocks, dtype=jnp.int32) * grid_rows + row_index
    slot_col = jnp.arange(col_blocks, dtype=jnp.int32) * grid_cols + col_index
    within = jnp.arange(window, dtype=jnp.int32)
    glob_row = (slot_row[:, None] * window + within[None, :]).reshape(rows_here)
    glob_col = (slot_col[:, None] * window + within[None, :]).reshape(cols_here)
    current = hessenberg
    for phase_idx in range(phases):
        chosen = factors[phase_idx : phase_idx + 1]
        row_raw = lax.all_gather(chosen, "col", axis=2, tiled=True)[0]
        gathered = lax.all_gather(chosen, "row", axis=1, tiled=True)
        col_raw = lax.all_to_all(
            sort_columns(gathered, grid_rows), "col", split_axis=1, concat_axis=3, tiled=True
        )
        col_raw = col_raw.reshape(col_blocks, window, window)
        flag_all = active[phase_idx]
        row_flag = jnp.take(flag_all, slot_row)
        col_flag = jnp.take(flag_all, slot_col)
        if phase_idx % 2 == 1:
            row_flag = jnp.where(slot_row < all_blocks - 1, row_flag, 0)
            col_flag = jnp.where(slot_col < all_blocks - 1, col_flag, 0)
        row_factor = effective(row_raw, row_flag)
        col_factor = effective(col_raw, col_flag)
        blocks = current.reshape(row_blocks, window, cols_here)
        if phase_idx % 2 == 0:
            updated = left_apply(row_factor, blocks)
            keep_mask = glob_col[None, :] >= (slot_row[:, None] + 1) * window
            current = jnp.where(keep_mask[:, None, :], updated, blocks).reshape(
                rows_here, cols_here
            )
            columns = current.reshape(rows_here, col_blocks, window)
            updated = right_apply(columns, col_factor)
            keep_mask = glob_row[:, None] < slot_col[None, :] * window
            current = jnp.where(keep_mask[:, :, None], updated, columns).reshape(
                rows_here, cols_here
            )
        else:
            top_half = blocks[:, :half_win]
            bottoms = blocks[:, half_win:]
            from_below = wrap_fix(
                passed_along(top_half, "row", -1), row_index == grid_rows - 1, -1, 0
            )
            stacked = jnp.concatenate([bottoms, from_below], axis=1)
            updated = left_apply(row_factor, stacked)
            keep_mask = glob_col[None, :] >= slot_row[:, None] * window + window + half_win
            updated = jnp.where(keep_mask[:, None, :], updated, stacked)
            returned = wrap_fix(passed_along(updated[:, half_win:], "row", 1), row_index == 0, 1, 0)
            current = jnp.concatenate([returned, updated[:, :half_win]], axis=1).reshape(
                rows_here, cols_here
            )
            columns = current.reshape(rows_here, col_blocks, window)
            left_half = columns[:, :, :half_win]
            right_half = columns[:, :, half_win:]
            from_right = wrap_fix(
                passed_along(left_half, "col", -1), col_index == grid_cols - 1, -1, 1
            )
            stacked = jnp.concatenate([right_half, from_right], axis=2)
            updated = right_apply(stacked, col_factor)
            keep_mask = glob_row[:, None] < slot_col[None, :] * window + half_win
            updated = jnp.where(keep_mask[:, :, None], updated, stacked)
            returned = wrap_fix(
                passed_along(updated[:, :, half_win:], "col", 1), col_index == 0, 1, 1
            )
            current = jnp.concatenate([returned, updated[:, :, :half_win]], axis=2).reshape(
                rows_here, cols_here
            )
    return current


def solution(mesh):
    return jax.shard_map(
        local,
        mesh=mesh,
        in_specs=(P("row", "col"), P(None, "row", "col", None), P()),
        out_specs=P("row", "col"),
        check_vma=False,
    )
```

profile of v0, /device:TPU:8, one launch (start us, length us, event | category | flops | bytes accessed | tf_op | source)
XLA Modules:
  0.0 635.5 jit_solution(7800001573734973021)
XLA Ops:
  6.5 1.9 slice_bitcast_fusion
  8.5 0.7 all-gather.17.cloned.1.call-update
  9.2 56.4 %all-gather.15.cloned.1.call-done = f32[1,32,32,512]{3,2,0,1:T(8,128)} async-done(((f32[1,2,32,512]{3,2,0,1:T(8,128)}), f32[1,32,32,512]{3,2,0,1:T(8,128)}) %all-gather.15.cloned.1.call-update) | async-done | bytes 2097168 | tf_op jit(solution)/shard_map/all_gather | solution.py:61
  65.6 8.6 %all-to-all-start.2 = ((f32[1,16,2,32,512]{4,3,2,0,1:T(8,128)}), f32[1,16,2,32,512]{4,3,2,0,1:T(8,128)S(1)}, u32[]{:S(2)}, u32[]{:S(2)}) async-start(f32[1,16,2,32,512]{4,3,2,0,1:T(8,128)} %bitcast.71), calls=%async_computation.2 | async-start | bytes 4194304 | tf_op jit(solution)/shard_map/all_to_all | solution.py:62
  74.3 0.7 all-gather.13.cloned.1.call-update
  75.2 0.6 gather_fusion.5
  75.9 0.6 gather_fusion.4
  76.8 90.4 %all-gather.17.cloned.1.call-done = f32[1,2,512,512]{3,2,1,0:T(8,128)} async-done(((f32[1,2,32,512]{3,2,1,0:T(8,128)}), f32[1,2,512,512]{3,2,1,0:T(8,128)}) %all-gather.17.cloned.1.call-update) | async-done | bytes 2097168 | tf_op jit(solution)/shard_map/all_gather | solution.py:60
  167.3 11.6 %convolution_select_fusion.1 = f32[2,512,1024]{2,1,0:T(8,128)} fusion(f32[2,512,1024]{2,1,0:T(8,128)} %bitcast.69, f32[1,2,512,512]{3,2,1,0:T(8,128)} %all-gather.17.cloned.1.call-done, pred[2,1024]{1,0:T(4,128)(4,1)S(1)} %get-tuple-element.30, f32[512,512]{1,0:T(8,128)S(1)} %fusion.20, pred[2]{0:T(512)(128)(4,1)S(1)} %select_compare_fusion), kind=kOutput, calls=%fused_computation.17 | convolution fusion | flops 6444023808 | bytes 11536386 | tf_op jit(solution)/shard_map/kab,kan->kbn/dot_general | solution.py:16
  178.9 6.6 %reshape_reshape.15 = f32[1024,2,512]{2,1,0:T(2,128)} reshape(f32[2,512,1024]{2,1,0:T(8,128)} %convolution_select_fusion.1) | data formatting | bytes 8388608 | tf_op jit(solution)/shard_map/reshape;reshape | solution.py:81
  185.5 7.2 %copy.56 = f32[1024,2,512]{0,2,1:T(8,128)} copy(f32[1024,2,512]{2,1,0:T(2,128)} %reshape_reshape.15) | data formatting | bytes 8388608 | tf_op jit(solution)/shard_map/reshape;reshape | solution.py:81
  192.7 0.2 copy.52
  192.9 2.0 copy-done
  194.9 8.8 %bitcast_select_fusion.2 = f32[1024,2,512]{0,2,1:T(8,128)} fusion(f32[1024,2,512]{0,2,1:T(8,128)S(1)} %copy-done, f32[2,512,512]{2,1,0:T(8,128)S(1)} %bitcast.67, pred[1024,2]{0,1:T(4,128)(4,1)S(1)} %get-tuple-element.28, f32[512,512]{1,0:T(8,128)S(1)} %fusion.20, pred[2]{0:T(512)(128)(4,1)S(1)} %select_compare_fusion.1), kind=kOutput, calls=%fused_computation.12 | convolution fusion | flops 6444023808 | bytes 11536386 | tf_op jit(solution)/shard_map/nka,kab->nkb/dot_general | solution.py:20
  203.7 6.6 %reshape_reshape.16 = f32[2,512,1024]{1,0,2:T(2,128)} reshape(f32[1024,2,512]{0,2,1:T(8,128)} %bitcast_select_fusion.2) | data formatting | bytes 8388608 | tf_op jit(solution)/shard_map/reshape;reshape | solution.py:74
  210.2 5.0 fusion.30
  215.2 2.9 copy.79
  218.1 0.2 collective-permute-start
  218.3 0.6 gather_fusion.3
  219.0 4.1 copy.78
  223.1 20.7 %collective-permute-done = f32[2,256,1024]{2,1,0:T(8,128)S(1)} collective-permute-done((f32[2,256,1024]{2,1,0:T(8,128)}, f32[2,256,1024]{2,1,0:T(8,128)S(1)}, u32[]{:S(2)}, u32[]{:S(2)}) %collective-permute-start) | collective-permute-done | bytes 2097184 | tf_op jit(solution)/shard_map/ppermute | solution.py:12
  243.9 0.1 fusion.34
  244.0 1.2 copy-done.1
  245.2 1.8 maximum_select_fusion
  247.0 10.6 %fusion.1 = f32[2,512,1024]{2,1,0:T(8,128)S(1)} fusion(f32[2,256,1024]{2,1,0:T(8,128)S(1)} %maximum_select_fusion, f32[2,256,1024]{2,1,0:T(8,128)} %copy.78, pred[2,1024]{1,0:T(4,128)(4,1)S(1)} %get-tuple-element.29, f32[1,2,512,512]{3,2,1,0:T(8,128)} %all-gather.13.cloned.1.call-done, f32[512,512]{1,0:T(8,128)S(1)} %fusion.20, pred[2]{0:T(512)(128)(4,1)S(1)} %fusion.22), kind=kOutput, calls=%fused_computation.14 | convolution fusion | flops 6446120960 | bytes 11536386 | tf_op jit(solution)/shard_map/kab,kan->kbn/dot_general | solution.py:16
  257.7 2.3 fusion.29
  260.1 60.6 %all-gather.11.cloned.1.call-done = f32[1,32,32,512]{3,2,0,1:T(8,128)} async-done(((f32[1,2,32,512]{3,2,0,1:T(8,128)}), f32[1,32,32,512]{3,2,0,1:T(8,128)}) %all-gather.11.cloned.1.call-update) | async-done | bytes 2097168 | tf_op jit(solution)/shard_map/all_gather | solution.py:61
  320.7 9.0 %all-to-all-start.1 = ((f32[1,16,2,32,512]{4,3,2,0,1:T(8,128)}), f32[1,16,2,32,512]{4,3,2,0,1:T(8,128)}, u32[]{:S(2)}, u32[]{:S(2)}) async-start(f32[1,16,2,32,512]{4,3,2,0,1:T(8,128)} %bitcast.72), calls=%async_computation.1 | async-start | bytes 4194304 | tf_op jit(solution)/shard_map/all_to_all | solution.py:62
  329.8 0.1 fusion.33
  329.9 0.4 maximum_select_fusion.1
  330.3 1.2 copy-done.4
  331.5 2.5 pad_maximum_fusion.1
  334.1 6.6 %reshape_reshape.17 = f32[1024,2,512]{2,1,0:T(2,128)} reshape(f32[2,512,1024]{2,1,0:T(8,128)} %pad_maximum_fusion.1) | data formatting | bytes 8388608 | tf_op jit(solution)/shard_map/reshape;reshape | solution.py:101
  340.6 5.0 fusion.28
  345.6 1.5 copy.81
  347.1 47.8 %all-gather.7.cloned.1.call-done = f32[1,32,32,512]{3,2,0,1:T(8,128)} async-done(((f32[1,2,32,512]{3,2,0,1:T(8,128)}), f32[1,32,32,512]{3,2,0,1:T(8,128)}) %all-gather.7.cloned.1.call-update) | async-done | bytes 2097168 | tf_op jit(solution)/shard_map/all_gather | solution.py:61
  395.0 47.3 %all-to-all-start = ((f32[1,16,2,32,512]{4,3,2,0,1:T(8,128)}), f32[1,16,2,32,512]{4,3,2,0,1:T(8,128)}, u32[]{:S(2)}, u32[]{:S(2)}) async-start(f32[1,16,2,32,512]{4,3,2,0,1:T(8,128)} %bitcast.70), calls=%async_computation | async-start | bytes 4194304 | tf_op jit(solution)/shard_map/all_to_all | solution.py:62
  442.3 0.5 all-gather.9.cloned.1.call-update
  442.9 0.6 gather_fusion.2
  443.5 2.0 copy.49
  445.5 0.2 copy-done.3
  445.7 0.2 copy.80
  445.9 0.1 fusion.32
  446.1 0.3 maximum_select_fusion.2
  446.3 7.8 %bitcast_select_fusion.1 = f32[1024,2,512]{2,0,1:T(8,128)S(1)} fusion(f32[1024,2,256]{2,0,1:T(8,128)S(1)} %maximum_select_fusion.2, f32[1024,2,256]{2,0,1:T(8,128)S(1)} %copy.80, pred[1024,2]{0,1:T(4,128)(4,1)S(1)} %get-tuple-element.27, f32[2,512,512]{2,1,0:T(8,128)S(1)} %bitcast.68, f32[512,512]{1,0:T(8,128)S(1)} %fusion.20, pred[2]{0:T(512)(128)(4,1)S(1)} %fusion.21), kind=kOutput, calls=%fused_computation.11 | convolution fusion | flops 6446120960 | bytes 11536386 | tf_op jit(solution)/shard_map/nka,kab->nkb/dot_general | solution.py:20
  454.1 2.4 fusion.27
  456.5 1.6 collective-permute-start.3
  458.1 0.6 gather_fusion.1
  458.8 0.6 gather_fusion
  459.4 36.7 %all-to-all-done = f32[1,16,2,32,512]{4,3,2,0,1:T(8,128)} async-done(((f32[1,16,2,32,512]{4,3,2,0,1:T(8,128)}), f32[1,16,2,32,512]{4,3,2,0,1:T(8,128)}, u32[]{:S(2)}, u32[]{:S(2)}) %all-to-all-start) | async-done | bytes 2097184 | tf_op jit(solution)/shard_map/all_to_all | solution.py:62
  496.2 3.3 copy.46
  499.4 43.7 %collective-permute-done.3 = f32[1024,2,256]{2,0,1:T(8,128)S(1)} collective-permute-done((f32[1024,2,256]{2,0,1:T(8,128)}, f32[1024,2,256]{2,0,1:T(8,128)S(1)}, u32[]{:S(2)}, u32[]{:S(2)}) %collective-permute-start.3) | collective-permute-done | bytes 2097184 | tf_op jit(solution)/shard_map/ppermute | solution.py:12
  543.1 0.1 fusion.31
  543.3 0.4 maximum_select_fusion.3
  543.7 1.2 copy-done.5
  544.8 0.6 pad_maximum_fusion.3
  545.5 5.3 copy.64
  550.7 6.6 %reshape_reshape.18 = f32[2,512,1024]{2,1,0:T(8,128)} reshape(f32[1024,2,512]{2,1,0:T(2,128)} %copy.64) | data formatting | bytes 8388608 | tf_op jit(solution)/shard_map/reshape;reshape | solution.py:74
  557.4 28.4 %all-gather.9.cloned.1.call-done = f32[1,2,512,512]{3,2,0,1:T(8,128)} async-done(((f32[1,2,32,512]{3,2,0,1:T(8,128)}), f32[1,2,512,512]{3,2,0,1:T(8,128)}) %all-gather.9.cloned.1.call-update) | async-done | bytes 2097168 | tf_op jit(solution)/shard_map/all_gather | solution.py:60
  585.8 11.6 %convolution_select_fusion = f32[2,512,1024]{2,1,0:T(8,128)} fusion(f32[2,512,1024]{2,1,0:T(8,128)} %reshape_reshape.18, f32[1,2,512,512]{3,2,0,1:T(8,128)} %all-gather.9.cloned.1.call-done, pred[2,1024]{1,0:T(4,128)(4,1)S(1)} %get-tuple-element.30, f32[512,512]{1,0:T(8,128)S(1)} %fusion.20, pred[2]{0:T(512)(128)(4,1)S(1)} %select_compare_fusion.2), kind=kOutput, calls=%fused_computation.16 | convolution fusion | flops 6444023808 | bytes 11536386 | tf_op jit(solution)/shard_map/kab,kan->kbn/dot_general | solution.py:16
  597.4 6.6 %reshape_reshape.19 = f32[1024,2,512]{2,1,0:T(2,128)} reshape(f32[2,512,1024]{2,1,0:T(8,128)} %convolution_select_fusion) | data formatting | bytes 8388608 | tf_op jit(solution)/shard_map/reshape;reshape | solution.py:81
  603.9 7.3 %copy.68 = f32[1024,2,512]{0,2,1:T(8,128)} copy(f32[1024,2,512]{2,1,0:T(2,128)} %reshape_reshape.19) | data formatting | bytes 8388608 | tf_op jit(solution)/shard_map/reshape;reshape | solution.py:81
  611.3 11.9 %bitcast_select_fusion = f32[1024,2,512]{0,2,1:T(8,128)} fusion(f32[1024,2,512]{0,2,1:T(8,128)} %copy.68, f32[2,512,512]{2,1,0:T(8,128)S(1)} %bitcast.66, pred[1024,2]{0,1:T(4,128)(4,1)S(1)} %get-tuple-element.28, f32[512,512]{1,0:T(8,128)S(1)} %fusion.20, pred[2]{0:T(512)(128)(4,1)S(1)} %select_compare_fusion.3), kind=kOutput, calls=%fused_computation.10 | convolution fusion | flops 6444023808 | bytes 11536386 | tf_op jit(solution)/shard_map/nka,kab->nkb/dot_general | solution.py:20
  623.2 5.3 copy.69
  (45 shorter events, 1.0 us)
Async XLA Ops:
  6.5 59.1 %all-gather.15.cloned.1.call-start = ((), (), s32[]{:S(2)}) async-start(), calls=%async_computation.7 | async-start | bytes 2228224 | tf_op jit(solution)/shard_map/all_gather | solution.py:61
  8.4 158.8 %all-gather.17.cloned.1.call-start = ((), (), s32[]{:S(2)}) async-start(), calls=%async_computation.8 | async-start | bytes 2228224 | tf_op jit(solution)/shard_map/all_gather | solution.py:60
  65.6 9.6 %copy-start.6 = (s32[3,32]{1,0:T(4,128)S(1)}, s32[3,32]{1,0:T(4,128)}, u32[]{:S(2)}) copy-start(s32[3,32]{1,0:T(4,128)} %param.7) | copy-start | bytes 1156
  65.6 127.1 %all-to-all-start.2 = ((f32[1,16,2,32,512]{4,3,2,0,1:T(8,128)}), f32[1,16,2,32,512]{4,3,2,0,1:T(8,128)S(1)}, u32[]{:S(2)}, u32[]{:S(2)}) async-start(f32[1,16,2,32,512]{4,3,2,0,1:T(8,128)} %bitcast.71), calls=%async_computation.2 | async-start | bytes 4194304 | tf_op jit(solution)/shard_map/all_to_all | solution.py:62
  74.2 172.8 %all-gather.13.cloned.1.call-start = ((), (), s32[]{:S(2)}) async-start(), calls=%async_computation.6 | async-start | bytes 2228224 | tf_op jit(solution)/shard_map/all_gather | solution.py:60
  74.9 245.8 %all-gather.11.cloned.1.call-start = ((), (), s32[]{:S(2)}) async-start(), calls=%async_computation.5 | async-start | bytes 2228224 | tf_op jit(solution)/shard_map/all_gather | solution.py:61
  192.7 2.2 copy-start
  218.1 25.8 %collective-permute-start = (f32[2,256,1024]{2,1,0:T(8,128)}, f32[2,256,1024]{2,1,0:T(8,128)S(1)}, u32[]{:S(2)}, u32[]{:S(2)}) collective-permute-start(f32[2,256,1024]{2,1,0:T(8,128)} %copy.79), channel_id=1, source_target_pairs={{0,240},{16,0},{32,16},{48,32},{64,48},{80,64},{96,80},{112,96},{1... | collective-permute-start | bytes 6291464 | tf_op jit(solution)/shard_map/ppermute | solution.py:12
  218.3 176.7 %all-gather.7.cloned.1.call-start = ((), (), s32[]{:S(2)}) async-start(), calls=%async_computation.3 | async-start | bytes 2228224 | tf_op jit(solution)/shard_map/all_gather | solution.py:61
  243.9 1.3 copy-start.1
  260.0 69.8 %collective-permute-start.1 = (f32[2,256,1024]{2,1,0:T(8,128)}, f32[2,256,1024]{2,1,0:T(8,128)S(1)}, u32[]{:S(2)}, u32[]{:S(2)}) collective-permute-start(f32[2,256,1024]{2,1,0:T(8,128)} %get-tuple-element.10), channel_id=1, source_target_pairs={{0,16},{16,32},{32,48},{48,64},{64,80},{80,96},{96,112},{112,128},... | collective-permute-start | bytes 6291464 | tf_op jit(solution)/shard_map/ppermute | solution.py:12
  320.7 74.2 %all-to-all-start.1 = ((f32[1,16,2,32,512]{4,3,2,0,1:T(8,128)}), f32[1,16,2,32,512]{4,3,2,0,1:T(8,128)}, u32[]{:S(2)}, u32[]{:S(2)}) async-start(f32[1,16,2,32,512]{4,3,2,0,1:T(8,128)} %bitcast.72), calls=%async_computation.1 | async-start | bytes 4194304 | tf_op jit(solution)/shard_map/all_to_all | solution.py:62
  329.9 1.6 copy-start.4
  347.1 98.8 %collective-permute-start.2 = (f32[1024,2,256]{2,0,1:T(8,128)}, f32[1024,2,256]{2,0,1:T(8,128)S(1)}, u32[]{:S(2)}, u32[]{:S(2)}) collective-permute-start(f32[1024,2,256]{2,0,1:T(8,128)} %copy.81), channel_id=1, source_target_pairs={{0,15},{1,0},{2,1},{3,2},{4,3},{5,4},{6,5},{7,6},{8,7},{9,8},{10,9... | collective-permute-start | bytes 6291464 | tf_op jit(solution)/shard_map/ppermute | solution.py:12
  395.0 101.2 %all-to-all-start = ((f32[1,16,2,32,512]{4,3,2,0,1:T(8,128)}), f32[1,16,2,32,512]{4,3,2,0,1:T(8,128)}, u32[]{:S(2)}, u32[]{:S(2)}) async-start(f32[1,16,2,32,512]{4,3,2,0,1:T(8,128)} %bitcast.70), calls=%async_computation | async-start | bytes 4194304 | tf_op jit(solution)/shard_map/all_to_all | solution.py:62
  442.3 143.5 %all-gather.9.cloned.1.call-start = ((), (), s32[]{:S(2)}) async-start(), calls=%async_computation.4 | async-start | bytes 2228224 | tf_op jit(solution)/shard_map/all_gather | solution.py:60
  443.5 2.2 copy-start.3
  456.5 86.6 %collective-permute-start.3 = (f32[1024,2,256]{2,0,1:T(8,128)}, f32[1024,2,256]{2,0,1:T(8,128)S(1)}, u32[]{:S(2)}, u32[]{:S(2)}) collective-permute-start(f32[1024,2,256]{2,0,1:T(8,128)} %get-tuple-element.6), channel_id=1, source_target_pairs={{0,1},{1,2},{2,3},{3,4},{4,5},{5,6},{6,7},{7,8},{8,9},{9,10},{10,1... | collective-permute-start | bytes 6291464 | tf_op jit(solution)/shard_map/ppermute | solution.py:12
  543.2 1.6 copy-start.5
  603.9 7.3 %copy-start.2 = (f32[1,1,2,16,32,512]{5,4,3,2,1,0:T(8,128)S(1)}, f32[1,1,2,16,32,512]{5,4,3,2,1,0:T(8,128)}, u32[]{:S(2)}) copy-start(f32[1,1,2,16,32,512]{5,4,3,2,1,0:T(8,128)} %copy.46) | copy-start | bytes 6291460
Sparse Core Ops, SparseCore 0:
  10.1 55.4 all-gather.14
  67.4 99.8 all-gather.16
  169.1 70.7 all-gather.12
  242.4 78.2 all-gather.10
  323.3 71.6 all-gather.6
  444.6 141.1 all-gather.8
where the time goes:
time: 648 us; the launch traced here: 636 us
  waiting for transfers between devices  387 us (60%)
  local copies, waits for them, and re-layouts  98.9 us (15%)
  starting transfers between devices  67.1 us (10%)
  matrix products  62.3 us (10%)
  between operations  13.9 us (2%)
  other arithmetic  6.62 us (1%)
    all_gather x3, waiting for transfers between devices, local(): gathered = lax.all_gather(chosen, 'row', axis=1, tiled=True)  165 us
    all_gather x3, waiting for transfers between devices, local(): row_raw = lax.all_gather(chosen, 'col', axis=2, tiled=True)[0]  119 us
    all_to_all x3, starting transfers between devices, local(): lax.all_to_all(sort_columns(gathered, grid_rows), 'col', split_axis=1, co...  65 us
    ppermute x4, waiting for transfers between devices, passed_along(): return lax.ppermute(value, axis, pairs)  64.4 us
    all_to_all x3, waiting for transfers between devices, local(): lax.all_to_all(sort_columns(gathered, grid_rows), 'col', split_axis=1, co...  36.7 us
    another operation x5, local copies, waits for them, and re-layouts, local(): columns = current.reshape(rows_here, col_blocks, window)  34.3 us
    dot_general x3, matrix products, left_apply(): return jnp.einsum('kab,kan->kbn', factor, stacked, precision=PRECISE)  33.8 us
    dot_general x3, matrix products, right_apply(): return jnp.einsum('nka,kab->nkb', stacked, factor, precision=PRECISE)  28.4 us
  transfers between devices with their start and end apart: 13, of which 8 were waited for; matrix products, arithmetic and copies ran while one was open for 18% of the time, Pallas kernels for 0%

commit v1 on v0

v1 whole, which is shorter than its diff:
```python
import functools

import jax
import jax.numpy as jnp
from jax import lax
from jax.experimental import pallas as pl
from jax.experimental.pallas import tpu as pltpu
from jax.sharding import PartitionSpec as P

MESH = pl.DeviceIdType.MESH
WIN = 512
HALF = 256
ROWS = 32
F32 = jnp.float32
BF16 = jnp.bfloat16
WINDOWS = ((0, 1), (0, 0), (1, 1))


def at(start, size):
    if isinstance(start, int):
        return pl.ds(start, size)
    return pl.ds(pl.multiple_of(start, size), size)


def unless(cond):
    return pl.when(jnp.logical_not(cond))


def kernel(
    flags, hess, fac, out,
    m1, m2, rf, cf, ta, s12, s21, s22, sh, zbuf, zhalf,
    lt_hi, lt_lo, r_hi, r_lo, w_hi, w_lo,
    ssem, rsem, lsem,
):
    r = lax.axis_index("row")
    c = lax.axis_index("col")
    core = r % 2
    x = (r // 2) % 4
    yh = r // 8
    yl = c % 2
    z = c // 2

    def row_of(xx):
        return yh * 8 + 2 * (xx % 4) + core

    xn, xp, xo = row_of(x + 1), row_of(x + 3), row_of(x + 2)
    zn, zp = (c + 2) % 16, (c + 14) % 16
    c_pair = c + 1 - 2 * yl
    r_pair = r + 1 - 2 * core
    r_far = (r + 8) % 16
    rm, rp = (r + 15) % 16, (r + 1) % 16
    cm, cp = (c + 15) % 16, (c + 1) % 16
    holder = yh == z // 4

    def scatter_target(xs):
        return (yh * 8 + 2 * x + yl, 2 * (4 * yh + xs) + core)

    def scatter_self(xs):
        return (core == yl) & (4 * yh + xs == z)

    bar = pltpu.get_barrier_semaphore()

    def greet(dev):
        pl.semaphore_signal(bar, inc=1, device_id=dev, device_id_type=MESH)

    for dev in (
        (r, c_pair), (r, zn), (r, zp), (r, cm), (r, cp),
        (r_pair, c), (r_far, c), (xn, c), (xp, c), (xo, c), (rm, c), (rp, c),
        (rm, cm), (rp, cp),
    ):
        greet(dev)
    for zz in range(8):
        own = (core == yl) & (zz == z)

        @pl.when(holder & jnp.logical_not(own))
        def _(zz=zz):
            greet((yh * 8 + 2 * x + yl, 2 * zz + core))

    self_target = holder & (core == yl)

    @pl.when(self_target)
    def _():
        pl.semaphore_wait(bar, 17)

    @unless(self_target)
    def _():
        pl.semaphore_wait(bar, 18)

    counts = [0, 0, 0]
    ends = []

    def take(which, n=1):
        first = counts[which]
        counts[which] += n
        return first

    def remote(src, dst, dev, cond=None):
        i = take(0)
        k = take(1)
        d = pltpu.make_async_remote_copy(
            src_ref=src, dst_ref=dst, send_sem=ssem.at[i], recv_sem=rsem.at[k],
            device_id=dev, device_id_type=MESH,
        )
        if cond is None:
            ends.append(d.wait_send)
        else:
            ends.append(lambda: pl.when(cond)(d.wait_send))
        return d

    def local(src, dst):
        i = take(2)
        return pltpu.make_async_copy(src, dst, lsem.at[i])

    load1 = local(hess, m1)
    load2 = local(hess, m2)
    load1.start()
    load2.start()

    def piece(f, q):
        return rf.at[f, :, at(q * ROWS, ROWS), :]

    def piece_k(f, k, q):
        return rf.at[f, k, at(q * ROWS, ROWS), :]

    def chunk(f, xx, kappa):
        return cf.at[f, xx // 2, :, kappa, xx % 2]

    def chunk_part(f, xx, kappa, part):
        return cf.at[f, xx // 2, pl.ds(4 * part, 4), kappa, xx % 2]

    dirs = (("p", zn, -1), ("m", zp, 1))
    Y, Z, A, B, G, C, own_rf, own_ta, own_cf = {}, {}, {}, {}, {}, {}, {}, {}, {}

    def own_sends(f):
        src = fac.at[f]
        Y[f] = remote(src, piece(f, c), (r, c_pair))
        Y[f].start()
        for name, dev, _ in dirs:
            Z[f, name, 0, 1] = remote(src, piece(f, c), (r, dev))
            Z[f, name, 0, 1].start()
        for d in (1, 2, 3):
            j = (x + d) % 4
            A[f, d] = remote(fac.at[f, j // 2, at((j % 2) * 16, 16), :], ta.at[f, x], (row_of(j), c))
            A[f, d].start()
        own_ta[f] = local(fac.at[f, x // 2, at((x % 2) * 16, 16), :], ta.at[f, x])
        own_ta[f].start()
        own_rf[f] = local(src, piece(f, c))
        own_rf[f].start()

    def pair_step(f):
        Y[f].wait_recv()
        for name, dev, _ in dirs:
            Z[f, name, 1, 1] = remote(piece(f, c_pair), piece(f, c_pair), (r, dev))
            Z[f, name, 1, 1].start()

    def z_step(f, hop):
        for s in (0, 1):
            for name, dev, sign in dirs:
                Z[f, name, s, hop].wait_recv()
                q = ((c if s == 0 else c_pair) + 2 * sign * hop + 16) % 16
                if hop < 3:
                    ref = piece(f, q)
                elif hop == 3:
                    ref = piece_k(f, 0 if name == "p" else 1, q)
                else:
                    continue
                Z[f, name, s, hop + 1] = remote(ref, ref, (r, dev))
                Z[f, name, s, hop + 1].start()

    def scatter_step(f):
        for d in (1, 2, 3):
            A[f, d].wait_recv()
        own_ta[f].wait()
        first = take(1, 8)
        own_cf[f] = local(ta.at[f, z % 4], cf.at[f, x // 2, z, yl, x % 2])
        for xs in range(4):
            i = take(0)
            d = pltpu.make_async_remote_copy(
                src_ref=ta.at[f, xs], dst_ref=cf.at[f, x // 2, z, yl, x % 2],
                send_sem=ssem.at[i], recv_sem=rsem.at[first + z],
                device_id=scatter_target(xs), device_id_type=MESH,
            )
            B[f, xs] = d
            unless(scatter_self(xs))(d.start)
            ends.append(lambda d=d, xs=xs: unless(scatter_self(xs))(d.wait_send))
        pl.when(self_target)(own_cf[f].start)
        B[f, "first"] = first

    def spread_step(f):
        first = B[f, "first"]
        mine = chunk(f, x, core)
        G[f, "far"] = remote(mine, mine, (r_far, c), holder)

        @pl.when(holder)
        def _():
            pl.when(self_target)(own_cf[f].wait)
            for zz in range(8):
                def arrived(zz=zz):
                    slot = cf.at[f, x // 2, zz, core, x % 2]
                    pltpu.make_async_remote_copy(
                        src_ref=slot, dst_ref=slot, send_sem=ssem.at[0], recv_sem=rsem.at[first + zz],
                        device_id=(r_far, c), device_id_type=MESH,
                    ).wait_recv()

                unless((core == yl) & (zz == z))(arrived)
            G[f, "far"].start()

        unless(holder)(G[f, "far"].wait_recv)
        for name, dev in (("p", xn), ("m", xp)):
            G[f, name, 1] = remote(mine, mine, (dev, c))
            G[f, name, 1].start()
        C[f, 0] = remote(mine, mine, (r_pair, c))
        C[f, 0].start()

    def x_step(f):
        for i, (name, dev, xs) in enumerate((("p", xn, (x + 3) % 4), ("m", xp, (x + 1) % 4))):
            G[f, name, 1].wait_recv()
            part = chunk_part(f, xs, core, i)
            G[f, name, 2] = remote(part, part, (dev, c))
            G[f, name, 2].start()
            got = chunk(f, xs, core)
            C[f, 1 + i] = remote(got, got, (r_pair, c))
            C[f, 1 + i].start()

    def x_last(f):
        for name in "pm":
            G[f, name, 2].wait_recv()
        got = chunk(f, (x + 2) % 4, core)
        C[f, 3] = remote(got, got, (r_pair, c))
        C[f, 3].start()

    def core_last(f):
        for i in range(4):
            C[f, i].wait_recv()
        own_rf[f].wait()

    def split(value):
        hi = value.astype(BF16)
        return hi, (value - hi.astype(F32)).astype(BF16)

    def dot(a, b):
        return jnp.dot(a, b, preferred_element_type=F32)

    def prepare(f):
        rows_i = lax.broadcasted_iota(jnp.int32, (WIN, WIN), 0)
        cols_i = lax.broadcasted_iota(jnp.int32, (WIN, WIN), 1)
        unit = (rows_i == cols_i).astype(F32)
        for k in range(2):
            on = jnp.full((WIN, WIN), flags[f, r + 16 * k], jnp.int32) > 0
            q = jnp.where(on, rf[f, k], unit)
            lt_hi[k], lt_lo[k] = split(q.T)
        for l in range(2):
            flag = flags[f, c + 16 * l]
            if f == 1 and l == 1:
                flag = flag * (c < 15).astype(jnp.int32)
            on = jnp.full((WIN, WIN), flag, jnp.int32) > 0
            q = jnp.where(on, cf[f, l].reshape(WIN, WIN), unit)
            r_hi[l], r_lo[l] = split(q)

    def right(rows, l):
        hi, lo = w_hi[0:rows], w_lo[0:rows]
        return dot(hi, r_hi[l]) + dot(hi, r_lo[l]) + dot(lo, r_hi[l])

    def both_sides(k, l):
        hi, lo = w_hi[...], w_lo[...]
        y = dot(lt_hi[k], hi) + dot(lt_hi[k], lo) + dot(lt_lo[k], hi)
        w_hi[...], w_lo[...] = split(y)
        return right(WIN, l)

    def above(k, l):
        return r + 16 * k < c + 16 * l

    def even_block(buf, k, l):
        @pl.when(above(k, l))
        def _():
            rs, cs = pl.ds(k * WIN, WIN), pl.ds(l * WIN, WIN)
            w_hi[...], w_lo[...] = split(buf[rs, cs])
            buf[rs, cs] = both_sides(k, l)

    l_wrap = (c == 0).astype(jnp.int32)
    k_wrap = (r == 0).astype(jnp.int32)
    l_over = (c == 15).astype(jnp.int32)
    k_over = (r == 15).astype(jnp.int32)

    def flip(slot, by):
        return slot + by * (1 - 2 * slot)

    def quad(buf, row, col):
        return buf.at[at(row, HALF), at(col, HALF)]

    def ends_before(dev_c, l):
        return dev_c + 16 * l < 31

    send, give_cond, take_cond, back = {}, {}, {}, {}

    def plan_out():
        for w, (k, l) in enumerate(WINDOWS):
            ks, ls = flip(k, k_wrap), flip(l, l_wrap)
            give_cond["12", w] = (r + 16 * k < cm + 16 * l) & ends_before(cm, l)
            give_cond["21", w] = rm + 16 * k < c + 16 * l
            give_cond["22", w] = (rm + 16 * k < cm + 16 * l) & ends_before(cm, l)
            take_cond["12", w] = above(k, l) & ends_before(c, l)
            take_cond["21", w] = above(k, l)
            take_cond["22", w] = take_cond["12", w]
            place = {
                "12": (k * WIN + HALF, ls * WIN, s12, (r, cm)),
                "21": (ks * WIN, l * WIN + HALF, s21, (rm, c)),
                "22": (ks * WIN, ls * WIN, s22, (rm, cm)),
            }
            for kind, (row, col, dst, dev) in place.items():
                send[kind, w] = remote(quad(m1, row, col), dst.at[w], dev, give_cond[kind, w])
        for l in range(2):
            give_cond["h", l] = (r == 0) & ends_before(cm, l)
            take_cond["h", l] = (r == 0) & ends_before(c, l)
            send["h", l] = remote(
                quad(m1, 0, flip(l, l_wrap) * WIN), sh.at[l], (r, cm), give_cond["h", l]
            )

    def give(kind, w, also=None):
        cond = give_cond[kind, w]
        pl.when(cond if also is None else cond & also)(send[kind, w].start)

    def got(kind, w):
        pl.when(take_cond[kind, w])(send[kind, w].wait_recv)

    def plan_back():
        for w, (k, l) in enumerate(WINDOWS):
            kr, lr = flip(k, k_over), flip(l, l_over)
            place = {
                "12": (0, HALF, k * WIN + HALF, lr * WIN, (r, cp)),
                "21": (HALF, 0, kr * WIN, l * WIN + HALF, (rp, c)),
                "22": (HALF, HALF, kr * WIN, lr * WIN, (rp, cp)),
            }
            for kind, (row, col, drow, dcol, dev) in place.items():
                src = zbuf.at[w, pl.ds(row, HALF), pl.ds(col, HALF)]
                back[kind, w] = remote(src, quad(m2, drow, dcol), dev, take_cond[kind, w])
        for l in range(2):
            back["h", l] = remote(
                zhalf.at[l, :, pl.ds(HALF, HALF)],
                quad(m2, 0, flip(l, l_over) * WIN), (r, cp), take_cond["h", l],
            )

    def odd_window(w):
        k, l = WINDOWS[w]
        for kind in ("12", "21", "22"):
            got(kind, w)

        @pl.when(above(k, l))
        def _():
            lo_half, hi_half = pl.ds(0, HALF), pl.ds(HALF, HALF)
            parts = (
                (lo_half, lo_half, m1[pl.ds(k * WIN + HALF, HALF), pl.ds(l * WIN + HALF, HALF)]),
                (lo_half, hi_half, s12[w]),
                (hi_half, lo_half, s21[w]),
                (hi_half, hi_half, s22[w]),
            )
            for rs, cs, value in parts:
                w_hi[rs, cs], w_lo[rs, cs] = split(value)
            result = both_sides(k, l)
            zbuf[w] = result
            m2[pl.ds(k * WIN + HALF, HALF), pl.ds(l * WIN + HALF, HALF)] = result[:HALF, :HALF]
            for kind in ("12", "21", "22"):
                pl.when(take_cond[kind, w])(back[kind, w].start)

    def top_window(l):
        got("h", l)

        @pl.when(take_cond["h", l])
        def _():
            top = pl.ds(0, HALF)
            w_hi[top, pl.ds(0, HALF)], w_lo[top, pl.ds(0, HALF)] = split(
                m1[top, pl.ds(l * WIN + HALF, HALF)]
            )
            w_hi[top, pl.ds(HALF, HALF)], w_lo[top, pl.ds(HALF, HALF)] = split(sh[l])
            result = right(HALF, l)
            zhalf[l] = result
            m2[top, pl.ds(l * WIN + HALF, HALF)] = result[:, :HALF]
            back["h", l].start()

    def unmoved():
        for k, l in WINDOWS:
            @pl.when(r + 16 * k + 1 == c + 16 * l)
            def _(k=k, l=l):
                rs, cs = pl.ds(k * WIN + HALF, HALF), pl.ds(l * WIN, HALF)
                m2[rs, cs] = m1[rs, cs]

        @pl.when((r == 0) & (c == 15))
        def _():
            rs, cs = pl.ds(0, HALF), pl.ds(WIN + HALF, HALF)
            m2[rs, cs] = m1[rs, cs]

    own_sends(0)
    plan_out()
    plan_back()

    @pl.when(c == 15)
    def _():
        for w in (0, 2):
            s12[w] = jnp.zeros((HALF, HALF), F32)
            s22[w] = jnp.zeros((HALF, HALF), F32)

    pair_step(0)
    scatter_step(0)
    z_step(0, 1)
    spread_step(0)
    own_sends(1)
    z_step(0, 2)
    x_step(0)
    z_step(0, 3)
    x_last(0)
    pair_step(1)
    scatter_step(1)
    z_step(0, 4)
    core_last(0)
    load1.wait()
    load2.wait()
    prepare(0)
    low = r > 0
    for l in range(2):
        pass
    even_block(m1, 0, 1)
    give("12", 0)
    give("21", 0, low)
    give("22", 0, low)
    z_step(1, 1)
    spread_step(1)
    even_block(m1, 0, 0)
    give("h", 0)
    give("h", 1)
    for kind in ("12", "21", "22"):
        give(kind, 1)
    z_step(1, 2)
    x_step(1)
    even_block(m1, 1, 1)
    give("21", 0, r == 0)
    give("22", 0, r == 0)
    for kind in ("12", "21", "22"):
        give(kind, 2)
    unmoved()
    own_sends(2)
    z_step(1, 3)
    x_last(1)
    z_step(1, 4)
    core_last(1)
    prepare(1)
    pair_step(2)
    scatter_step(2)
    odd_window(0)
    z_step(2, 1)
    spread_step(2)
    for l in range(2):
        top_window(l)
    odd_window(1)
    z_step(2, 2)
    x_step(2)
    odd_window(2)
    z_step(2, 3)
    x_last(2)
    z_step(2, 4)
    core_last(2)
    prepare(2)
    for key, cond in give_cond.items():
        pl.when(cond)(back[key].wait_recv)
    stores = []
    for k, l in ((1, 0),) + WINDOWS:
        if (k, l) != (1, 0):
            even_block(m2, k, l)
        rs, cs = pl.ds(k * WIN, WIN), pl.ds(l * WIN, WIN)
        d = local(m2.at[rs, cs], out.at[rs, cs])
        d.start()
        stores.append(d)
    for end in ends:
        end()
    for d in stores:
        d.wait()


def local(hessenberg, factors, active):
    sems = 150
    return pl.pallas_call(
        kernel,
        out_shape=jax.ShapeDtypeStruct(hessenberg.shape, F32),
        in_specs=[
            pl.BlockSpec(memory_space=pltpu.SMEM),
            pl.BlockSpec(memory_space=pl.ANY),
            pl.BlockSpec(memory_space=pl.ANY),
        ],
        out_specs=pl.BlockSpec(memory_space=pl.ANY),
        scratch_shapes=[
            pltpu.VMEM((1024, 1024), F32),
            pltpu.VMEM((1024, 1024), F32),
            pltpu.VMEM((3, 2, WIN, WIN), F32),
            pltpu.VMEM((3, 2, 8, 2, 2, 16, WIN), F32),
            pltpu.VMEM((3, 4, 16, WIN), F32),
            pltpu.VMEM((3, HALF, HALF), F32),
            pltpu.VMEM((3, HALF, HALF), F32),
            pltpu.VMEM((3, HALF, HALF), F32),
            pltpu.VMEM((2, HALF, HALF), F32),
            pltpu.VMEM((3, WIN, WIN), F32),
            pltpu.VMEM((2, HALF, WIN), F32),
            pltpu.VMEM((2, WIN, WIN), BF16),
            pltpu.VMEM((2, WIN, WIN), BF16),
            pltpu.VMEM((2, WIN, WIN), BF16),
            pltpu.VMEM((2, WIN, WIN), BF16),
            pltpu.VMEM((WIN, WIN), BF16),
            pltpu.VMEM((WIN, WIN), BF16),
            pltpu.SemaphoreType.DMA((sems,)),
            pltpu.SemaphoreType.DMA((sems,)),
            pltpu.SemaphoreType.DMA((16,)),
        ],
        compiler_params=pltpu.CompilerParams(
            collective_id=0, has_side_effects=True, vmem_limit_bytes=56 << 20
        ),
        name="sweep",
    )(active, hessenberg, factors)


def solution(mesh):
    return jax.shard_map(
        local,
        mesh=mesh,
        in_specs=(P("row", "col"), P(None, "row", "col", None), P()),
        out_specs=P("row", "col"),
        check_vma=False,
    )
```

time: 648 us -> 178 us (0.27)
  the two profiles are of different devices: /device:TPU:8 before, /device:TPU:72 now
where the time goes in v1:
time: 178 us; the launch traced here: 177 us
  Pallas kernels  173 us (97%)
  local copies, waits for them, and re-layouts  4.79 us (3%)
    pallas_call x1, Pallas kernels, local(): pl.pallas_call(kernel, out_shape=jax.ShapeDtypeStruct(hessenberg.shape, F...  173 us
    unnamed x1, local copies, waits for them, and re-layouts  4.79 us

profile of v1, /device:TPU:72, one launch (start us, length us, event | category | flops | bytes accessed | tf_op | source)
XLA Modules:
  0.0 177.4 jit_solution(11145773303435942360)
XLA Ops:
  0.0 172.6 %sweep.1 = f32[1024,1024]{1,0:T(8,128)} custom-call(s32[3,32]{1,0:T(4,128)} %flags.1, f32[1024,1024]{1,0:T(8,128)} %hess.1, f32[3,2,32,512]{3,2,1,0:T(8,128)} %fac.1), custom_call_target="tpu_custom_call" | custom-call | tf_op jit(solution)/shard_map/sweep/pallas_call | solution.py:480
  172.6 4.8 %copy.5 = f32[1024,1024]{1,0:T(8,128)} copy(f32[1024,1024]{1,0:T(8,128)} %sweep.1) | data formatting | bytes 8388608

commit v2 on v1

v2 whole, which is shorter than its diff:
```python
import functools

import jax
import jax.numpy as jnp
from jax import lax
from jax.experimental import pallas as pl
from jax.experimental.pallas import tpu as pltpu
from jax.sharding import PartitionSpec as P

MESH = pl.DeviceIdType.MESH
WIN = 512
HALF = 256
ROWS = 32
F32 = jnp.float32
BF16 = jnp.bfloat16
WINDOWS = ((0, 1), (0, 0), (1, 1))


PLAN = (
    ("cf", 0), ("y", 0), ("rf", 0), ("scatter", 0), ("y", 1), ("y", 2), ("cf", 1), ("cf", 2), ("pair", 0), ("far", 0),
    ("z", 0, 1), ("line", 0), ("z", 0, 2), ("x", 0), ("scatter", 1), ("z", 0, 3), ("xlast", 0), ("scatter", 2),
    ("z", 0, 4), ("far", 1), ("rf", 1), ("pair", 1),
    ("clear",), ("loaded",), ("pleft", 0), ("left0", 0), ("left0", 1), ("left0", 2), ("far", 2), ("pairlast", 0),
    ("pright", 0), ("block0", 0), ("block0", 1), ("block0", 2),
    ("z", 1, 1), ("line", 1), ("z", 1, 2), ("x", 1), ("z", 1, 3), ("xlast", 1), ("z", 1, 4), ("pairlast", 1),
    ("rf", 2), ("pair", 2), ("pleft", 1), ("pright", 1), ("odd", 0), ("top", 0), ("top", 1), ("odd", 1), ("odd", 2),
    ("z", 2, 1), ("line", 2), ("z", 2, 2), ("x", 2), ("z", 2, 3), ("xlast", 2), ("z", 2, 4), ("pairlast", 2),
    ("pleft", 2), ("pright", 2),
    ("returned",), ("block2", 1, 0), ("block2", 0, 1), ("block2", 0, 0), ("block2", 1, 1),
)


def at(start, size):
    if isinstance(start, int):
        return pl.ds(start, size)
    return pl.ds(pl.multiple_of(start, size), size)


def unless(cond):
    return pl.when(jnp.logical_not(cond))


def kernel(
    flags, hess, fac, out,
    m1, m2, rf, cf, ta, s12, s21, s22, sh, zbuf, zhalf,
    lt_hi, lt_lo, r_hi, r_lo, w_hi, w_lo, y_hi, y_lo,
    ssem, rsem, lsem,
):
    r = lax.axis_index("row")
    c = lax.axis_index("col")
    core = r % 2
    x = (r // 2) % 4
    yh = r // 8
    yl = c % 2
    z = c // 2

    def row_of(xx):
        return yh * 8 + 2 * (xx % 4) + core

    xn, xp = row_of(x + 1), row_of(x + 3)
    zn, zp = (c + 2) % 16, (c + 14) % 16
    c_pair = c + 1 - 2 * yl
    r_pair = r + 1 - 2 * core
    r_far = (r + 8) % 16
    rm, rp = (r + 15) % 16, (r + 1) % 16
    cm, cp = (c + 15) % 16, (c + 1) % 16
    spot = yh * 4 + x
    mirrored = core == yl

    def chip_row(t):
        return t // 4 * 8 + t % 4 * 2 + core

    def scatter_to(zz):
        return (yh * 8 + 2 * x + yl, 2 * zz + core)

    load1 = pltpu.make_async_copy(hess, m1, lsem.at[0])
    load2 = pltpu.make_async_copy(hess, m2, lsem.at[1])
    load1.start()
    load2.start()

    bar = pltpu.get_barrier_semaphore()

    def greet(dev):
        pl.semaphore_signal(bar, inc=1, device_id=dev, device_id_type=MESH)

    for dev in (
        (r, zn), (r, zp), (r, cm), (r, cp), (rm, c), (rp, c), (rm, cm), (rp, cp),
    ):
        greet(dev)
    for step in range(1, 8):
        greet((chip_row((spot + step) % 8), c))
    for zz in range(8):
        unless(mirrored & (zz == z))(functools.partial(greet, scatter_to(zz)))
    pl.when(mirrored)(lambda: pl.semaphore_wait(bar, 22))
    unless(mirrored)(lambda: pl.semaphore_wait(bar, 23))

    counts = [0, 0, 2]
    ends = []

    def take(which, n=1):
        first = counts[which]
        counts[which] += n
        return first

    def remote(src, dst, dev, cond=None):
        i = take(0)
        k = take(1)
        copy = pltpu.make_async_remote_copy(
            src_ref=src, dst_ref=dst, send_sem=ssem.at[i], recv_sem=rsem.at[k],
            device_id=dev, device_id_type=MESH,
        )
        if cond is None:
            ends.append(copy.wait_send)
        else:
            ends.append(lambda: pl.when(cond)(copy.wait_send))
        return copy

    def local(src, dst):
        i = take(2)
        return pltpu.make_async_copy(src, dst, lsem.at[i])

    def piece(f, q):
        return rf.at[f, :, at(q * ROWS, ROWS), :]

    def piece_k(f, k, q):
        return rf.at[f, k, at(q * ROWS, ROWS), :]

    def eighth(f, xx, kappa, e):
        return cf.at[f, xx // 2, :, kappa, xx % 2, e]

    def chunk(f, xx, kappa):
        return cf.at[f, xx // 2, :, kappa, xx % 2]

    def chunk_part(f, xx, kappa, part):
        return cf.at[f, xx // 2, pl.ds(4 * part, 4), kappa, xx % 2]

    dirs = (("p", zn, -1), ("m", zp, 1))
    Y, Z, A, B, G, C, own_rf, own_ta, own_cf = {}, {}, {}, {}, {}, {}, {}, {}, {}

    def own_pair(f):
        Y[f] = remote(fac.at[f], piece(f, c), (r, c_pair))
        Y[f].start()

    def own_row(f):
        src = fac.at[f]
        for name, dev, _ in dirs:
            Z[f, name, 0, 1] = remote(src, piece(f, c), (r, dev))
            Z[f, name, 0, 1].start()
        own_rf[f] = local(src, piece(f, c))
        own_rf[f].start()

    def own_col(f):
        def part(t):
            return fac.at[f, t % 4 // 2, at(t % 2 * 16 + t // 4 * 8, 8), :]

        for step in range(1, 8):
            t = (spot + step) % 8
            A[f, step] = remote(part(t), ta.at[f, spot], (chip_row(t), c))
            A[f, step].start()
        own_ta[f] = local(part(spot), ta.at[f, spot])
        own_ta[f].start()

    def pair_step(f):
        Y[f].wait_recv()
        own_rf[f].wait()
        for name, dev, _ in dirs:
            Z[f, name, 1, 1] = remote(piece(f, c_pair), piece(f, c_pair), (r, dev))
            Z[f, name, 1, 1].start()

    def z_step(f, hop):
        for s in (0, 1):
            for name, dev, sign in dirs:
                Z[f, name, s, hop].wait_recv()
                q = ((c if s == 0 else c_pair) + 2 * sign * hop + 16) % 16
                if hop < 3:
                    ref = piece(f, q)
                elif hop == 3:
                    ref = piece_k(f, 0 if name == "p" else 1, q)
                else:
                    continue
                Z[f, name, s, hop + 1] = remote(ref, ref, (r, dev))
                Z[f, name, s, hop + 1].start()

    def scatter_step(f):
        for step in range(1, 8):
            A[f, step].wait_recv()
        own_ta[f].wait()
        first = B[f] = take(1, 8)
        landing = eighth(f, x, yl, yh).at[z]
        own_cf[f] = local(ta.at[f, z], landing)
        for zz in range(8):
            copy = pltpu.make_async_remote_copy(
                src_ref=ta.at[f, zz], dst_ref=landing, send_sem=ssem.at[take(0)], recv_sem=rsem.at[first + z],
                device_id=scatter_to(zz), device_id_type=MESH,
            )
            home = mirrored & (zz == z)
            unless(home)(copy.start)
            ends.append(lambda copy=copy, home=home: unless(home)(copy.wait_send))
        pl.when(mirrored)(own_cf[f].start)

    def far_step(f):
        mine = eighth(f, x, core, yh)
        pl.when(mirrored)(own_cf[f].wait)
        for zz in range(8):
            slot = mine.at[zz]
            copy = pltpu.make_async_remote_copy(
                src_ref=slot, dst_ref=slot, send_sem=ssem.at[0], recv_sem=rsem.at[B[f] + zz],
                device_id=(r_far, c), device_id_type=MESH,
            )
            unless(mirrored & (zz == z))(copy.wait_recv)
        G[f, "far"] = remote(mine, mine, (r_far, c))
        G[f, "far"].start()

    def line_step(f):
        G[f, "far"].wait_recv()
        mine = chunk(f, x, core)
        for name, dev in (("p", xn), ("m", xp)):
            G[f, name, 1] = remote(mine, mine, (dev, c))
            G[f, name, 1].start()
        C[f, 0] = remote(mine, mine, (r_pair, c))
        C[f, 0].start()

    def x_step(f):
        for i, (name, dev, xs) in enumerate((("p", xn, (x + 3) % 4), ("m", xp, (x + 1) % 4))):
            G[f, name, 1].wait_recv()
            part = chunk_part(f, xs, core, i)
            G[f, name, 2] = remote(part, part, (dev, c))
            G[f, name, 2].start()
            got = chunk(f, xs, core)
            C[f, 1 + i] = remote(got, got, (r_pair, c))
            C[f, 1 + i].start()

    def x_last(f):
        for name in "pm":
            G[f, name, 2].wait_recv()
        got = chunk(f, (x + 2) % 4, core)
        C[f, 3] = remote(got, got, (r_pair, c))
        C[f, 3].start()

    def pair_last(f):
        for i in range(4):
            C[f, i].wait_recv()

    def split(value):
        hi = value.astype(BF16)
        return hi, (value - hi.astype(F32)).astype(BF16)

    def dot(a, b):
        return jnp.dot(a, b, preferred_element_type=F32)

    def unit():
        rows_i = lax.broadcasted_iota(jnp.int32, (WIN, WIN), 0)
        cols_i = lax.broadcasted_iota(jnp.int32, (WIN, WIN), 1)
        return (rows_i == cols_i).astype(F32)

    def prepare_left(f):
        for k in range(2):
            on = jnp.full((WIN, WIN), flags[f, r + 16 * k], jnp.int32) > 0
            lt_hi[k], lt_lo[k] = split(jnp.where(on, rf[f, k], unit()).T)

    def prepare_right(f):
        for l in range(2):
            flag = flags[f, c + 16 * l]
            if f == 1 and l == 1:
                flag = flag * (c < 15).astype(jnp.int32)
            on = jnp.full((WIN, WIN), flag, jnp.int32) > 0
            r_hi[l], r_lo[l] = split(jnp.where(on, cf[f, l].reshape(WIN, WIN), unit()))

    def times_right(hi, lo, l):
        return dot(hi, r_hi[l]) + dot(hi, r_lo[l]) + dot(lo, r_hi[l])

    def left(k, w):
        hi, lo = w_hi[...], w_lo[...]
        y_hi[w], y_lo[w] = split(dot(lt_hi[k], hi) + dot(lt_hi[k], lo) + dot(lt_lo[k], hi))

    def above(k, l):
        return r + 16 * k < c + 16 * l

    def place(w):
        k, l = WINDOWS[w]
        return pl.ds(k * WIN, WIN), pl.ds(l * WIN, WIN)

    def even_left(buf, w):
        k, l = WINDOWS[w]

        @pl.when(above(k, l))
        def _():
            w_hi[...], w_lo[...] = split(buf[place(w)])
            left(k, w)

    def even_right(buf, w):
        k, l = WINDOWS[w]

        @pl.when(above(k, l))
        def _():
            buf[place(w)] = times_right(y_hi[w], y_lo[w], l)

    l_wrap = (c == 0).astype(jnp.int32)
    k_wrap = (r == 0).astype(jnp.int32)
    l_over = (c == 15).astype(jnp.int32)
    k_over = (r == 15).astype(jnp.int32)

    def flip(slot, by):
        return slot + by * (1 - 2 * slot)

    def quad(buf, row, col):
        return buf.at[at(row, HALF), at(col, HALF)]

    def ends_before(dev_c, l):
        return dev_c + 16 * l < 31

    send, give_cond, take_cond, back = {}, {}, {}, {}

    def plan_out():
        for w, (k, l) in enumerate(WINDOWS):
            ks, ls = flip(k, k_wrap), flip(l, l_wrap)
            give_cond["12", w] = (r + 16 * k < cm + 16 * l) & ends_before(cm, l)
            give_cond["21", w] = rm + 16 * k < c + 16 * l
            give_cond["22", w] = (rm + 16 * k < cm + 16 * l) & ends_before(cm, l)
            take_cond["12", w] = above(k, l) & ends_before(c, l)
            take_cond["21", w] = above(k, l)
            take_cond["22", w] = take_cond["12", w]
            spots = {
                "12": (k * WIN + HALF, ls * WIN, s12, (r, cm)),
                "21": (ks * WIN, l * WIN + HALF, s21, (rm, c)),
                "22": (ks * WIN, ls * WIN, s22, (rm, cm)),
            }
            for kind, (row, col, dst, dev) in spots.items():
                send[kind, w] = remote(quad(m1, row, col), dst.at[w], dev, give_cond[kind, w])
        for l in range(2):
            give_cond["h", l] = (r == 0) & ends_before(cm, l)
            take_cond["h", l] = (r == 0) & ends_before(c, l)
            send["h", l] = remote(
                quad(m1, 0, flip(l, l_wrap) * WIN), sh.at[l], (r, cm), give_cond["h", l]
            )

    def give(kind, w, also=None):
        cond = give_cond[kind, w]
        pl.when(cond if also is None else cond & also)(send[kind, w].start)

    def got(kind, w):
        pl.when(take_cond[kind, w])(send[kind, w].wait_recv)

    def plan_back():
        for w, (k, l) in enumerate(WINDOWS):
            kr, lr = flip(k, k_over), flip(l, l_over)
            spots = {
                "12": (0, HALF, k * WIN + HALF, lr * WIN, (r, cp)),
                "21": (HALF, 0, kr * WIN, l * WIN + HALF, (rp, c)),
                "22": (HALF, HALF, kr * WIN, lr * WIN, (rp, cp)),
            }
            for kind, (row, col, drow, dcol, dev) in spots.items():
                src = zbuf.at[w, pl.ds(row, HALF), pl.ds(col, HALF)]
                back[kind, w] = remote(src, quad(m2, drow, dcol), dev, take_cond[kind, w])
        for l in range(2):
            back["h", l] = remote(
                zhalf.at[l, :, pl.ds(HALF, HALF)],
                quad(m2, 0, flip(l, l_over) * WIN), (r, cp), take_cond["h", l],
            )

    def odd_window(w):
        k, l = WINDOWS[w]
        for kind in ("12", "21", "22"):
            got(kind, w)

        @pl.when(above(k, l))
        def _():
            lo_half, hi_half = pl.ds(0, HALF), pl.ds(HALF, HALF)
            parts = (
                (lo_half, lo_half, m1[pl.ds(k * WIN + HALF, HALF), pl.ds(l * WIN + HALF, HALF)]),
                (lo_half, hi_half, s12[w]),
                (hi_half, lo_half, s21[w]),
                (hi_half, hi_half, s22[w]),
            )
            for rs, cs, value in parts:
                w_hi[rs, cs], w_lo[rs, cs] = split(value)
            left(k, w)
            result = times_right(y_hi[w], y_lo[w], l)
            zbuf[w] = result
            m2[pl.ds(k * WIN + HALF, HALF), pl.ds(l * WIN + HALF, HALF)] = result[:HALF, :HALF]
            for kind in ("12", "21", "22"):
                pl.when(take_cond[kind, w])(back[kind, w].start)

    def top_window(l):
        got("h", l)

        @pl.when(take_cond["h", l])
        def _():
            top = pl.ds(0, HALF)
            w_hi[top, pl.ds(0, HALF)], w_lo[top, pl.ds(0, HALF)] = split(
                m1[top, pl.ds(l * WIN + HALF, HALF)]
            )
            w_hi[top, pl.ds(HALF, HALF)], w_lo[top, pl.ds(HALF, HALF)] = split(sh[l])
            result = times_right(w_hi[top], w_lo[top], l)
            zhalf[l] = result
            m2[top, pl.ds(l * WIN + HALF, HALF)] = result[:, :HALF]
            back["h", l].start()

    def unmoved():
        for k, l in WINDOWS:
            @pl.when(r + 16 * k + 1 == c + 16 * l)
            def _(k=k, l=l):
                rs, cs = pl.ds(k * WIN + HALF, HALF), pl.ds(l * WIN, HALF)
                m2[rs, cs] = m1[rs, cs]

        @pl.when((r == 0) & (c == 15))
        def _():
            rs, cs = pl.ds(0, HALF), pl.ds(WIN + HALF, HALF)
            m2[rs, cs] = m1[rs, cs]

    plan_out()
    plan_back()

    def clear():
        @pl.when(c == 15)
        def _():
            for w in (0, 2):
                s12[w] = jnp.zeros((HALF, HALF), F32)
                s22[w] = jnp.zeros((HALF, HALF), F32)

    def loaded():
        load1.wait()
        load2.wait()

    def block0(w):
        even_right(m1, w)
        kinds = ("12", "21", "22")
        if w == 0:
            give("12", 0)
            give("21", 0, r > 0)
            give("22", 0, r > 0)
        elif w == 1:
            give("h", 0)
            give("h", 1)
            for kind in kinds:
                give(kind, 1)
        else:
            give("21", 0, r == 0)
            give("22", 0, r == 0)
            for kind in kinds:
                give(kind, 2)
            unmoved()

    def returned():
        for key, cond in give_cond.items():
            pl.when(cond)(back[key].wait_recv)

    stores = []

    def block2(k, l):
        if (k, l) in WINDOWS:
            even_left(m2, WINDOWS.index((k, l)))
            even_right(m2, WINDOWS.index((k, l)))
        rs, cs = pl.ds(k * WIN, WIN), pl.ds(l * WIN, WIN)
        copy = local(m2.at[rs, cs], out.at[rs, cs])
        copy.start()
        stores.append(copy)

    def left0(w):
        even_left(m1, w)

    steps = dict(
        y=own_pair, rf=own_row, cf=own_col, pair=pair_step, z=z_step, scatter=scatter_step, far=far_step, line=line_step, x=x_step,
        xlast=x_last, pairlast=pair_last, loaded=loaded, pleft=prepare_left,
        pright=prepare_right, left0=left0, block0=block0, clear=clear, odd=odd_window, top=top_window,
        returned=returned, block2=block2,
    )
    for name, *args in PLAN:
        steps[name](*args)
    for end in ends:
        end()
    for copy in stores:
        copy.wait()


def local(hessenberg, factors, active):
    sems = 160
    return pl.pallas_call(
        kernel,
        out_shape=jax.ShapeDtypeStruct(hessenberg.shape, F32),
        in_specs=[
            pl.BlockSpec(memory_space=pltpu.SMEM),
            pl.BlockSpec(memory_space=pl.ANY),
            pl.BlockSpec(memory_space=pl.ANY),
        ],
        out_specs=pl.BlockSpec(memory_space=pl.ANY),
        scratch_shapes=[
            pltpu.VMEM((1024, 1024), F32),
            pltpu.VMEM((1024, 1024), F32),
            pltpu.VMEM((3, 2, WIN, WIN), F32),
            pltpu.VMEM((3, 2, 8, 2, 2, 2, 8, WIN), F32),
            pltpu.VMEM((3, 8, 8, WIN), F32),
            pltpu.VMEM((3, HALF, HALF), F32),
            pltpu.VMEM((3, HALF, HALF), F32),
            pltpu.VMEM((3, HALF, HALF), F32),
            pltpu.VMEM((2, HALF, HALF), F32),
            pltpu.VMEM((3, WIN, WIN), F32),
            pltpu.VMEM((2, HALF, WIN), F32),
            pltpu.VMEM((2, WIN, WIN), BF16),
            pltpu.VMEM((2, WIN, WIN), BF16),
            pltpu.VMEM((2, WIN, WIN), BF16),
            pltpu.VMEM((2, WIN, WIN), BF16),
            pltpu.VMEM((WIN, WIN), BF16),
            pltpu.VMEM((WIN, WIN), BF16),
            pltpu.VMEM((3, WIN, WIN), BF16),
            pltpu.VMEM((3, WIN, WIN), BF16),
            pltpu.SemaphoreType.DMA((sems,)),
            pltpu.SemaphoreType.DMA((sems,)),
            pltpu.SemaphoreType.DMA((16,)),
        ],
        compiler_params=pltpu.CompilerParams(
            collective_id=0, has_side_effects=True, vmem_limit_bytes=56 << 20
        ),
        name="sweep",
    )(active, hessenberg, factors)


def solution(mesh):
    return jax.shard_map(
        local,
        mesh=mesh,
        in_specs=(P("row", "col"), P(None, "row", "col", None), P()),
        out_specs=P("row", "col"),
        check_vma=False,
    )
```

time: 178 us -> 165 us (0.927)
  the two profiles are of different devices: /device:TPU:72 before, /device:TPU:8 now
where the time goes in v2:
time: 165 us
  Pallas kernels  160 us (97%)
  local copies, waits for them, and re-layouts  4.79 us (3%)
    pallas_call x1, Pallas kernels, local(): pl.pallas_call(kernel, out_shape=jax.ShapeDtypeStruct(hessenberg.shape, F...  160 us
    unnamed x1, local copies, waits for them, and re-layouts  4.79 us

profile of v2, /device:TPU:8, one launch (start us, length us, event | category | flops | bytes accessed | tf_op | source)
XLA Modules:
  0.0 165.3 jit_solution(10661517622591195555)
XLA Ops:
  0.0 160.5 %sweep.1 = f32[1024,1024]{1,0:T(8,128)} custom-call(s32[3,32]{1,0:T(4,128)} %flags.1, f32[1024,1024]{1,0:T(8,128)} %hess.1, f32[3,2,32,512]{3,2,1,0:T(8,128)} %fac.1), custom_call_target="tpu_custom_call" | custom-call | tf_op jit(solution)/shard_map/sweep/pallas_call | solution.py:478
  160.5 4.8 %copy.5 = f32[1024,1024]{1,0:T(8,128)} copy(f32[1024,1024]{1,0:T(8,128)} %sweep.1) | data formatting | bytes 8388608

commit v3 on v2

--- a/solution.py
+++ b/solution.py
@@ -17,16 +17,15 @@
 
 
 PLAN = (
-    ("cf", 0), ("y", 0), ("rf", 0), ("scatter", 0), ("y", 1), ("y", 2), ("cf", 1), ("cf", 2), ("pair", 0), ("far", 0),
-    ("z", 0, 1), ("line", 0), ("z", 0, 2), ("x", 0), ("scatter", 1), ("z", 0, 3), ("xlast", 0), ("scatter", 2),
-    ("z", 0, 4), ("far", 1), ("rf", 1), ("pair", 1),
-    ("clear",), ("loaded",), ("pleft", 0), ("left0", 0), ("left0", 1), ("left0", 2), ("far", 2), ("pairlast", 0),
-    ("pright", 0), ("block0", 0), ("block0", 1), ("block0", 2),
-    ("z", 1, 1), ("line", 1), ("z", 1, 2), ("x", 1), ("z", 1, 3), ("xlast", 1), ("z", 1, 4), ("pairlast", 1),
-    ("rf", 2), ("pair", 2), ("pleft", 1), ("pright", 1), ("odd", 0), ("top", 0), ("top", 1), ("odd", 1), ("odd", 2),
-    ("z", 2, 1), ("line", 2), ("z", 2, 2), ("x", 2), ("z", 2, 3), ("xlast", 2), ("z", 2, 4), ("pairlast", 2),
-    ("pleft", 2), ("pright", 2),
-    ("returned",), ("block2", 1, 0), ("block2", 0, 1), ("block2", 0, 0), ("block2", 1, 1),
+    ("cf", 0), ("y", 0), ("rf", 0), ("scatter", 0), ("y", 1), ("y", 2), ("cf", 1), ("cf", 2), ("pair", 0),
+    ("far", 0), ("z", 0, 1), ("line", 0), ("z", 0, 2), ("x", 0), ("scatter", 1), ("z", 0, 3), ("xlast", 0),
+    ("scatter", 2), ("z", 0, 4), ("far", 1), ("clear",), ("loaded",), ("pleft", 0), ("left0", 0), ("left0", 1),
+    ("left0", 2), ("far", 2), ("pairlast", 0), ("pright", 0), ("rf", 1), ("pair", 1), ("line", 1), ("block0", 0),
+    ("block0", 1), ("block0", 2), ("z", 1, 1), ("z", 1, 2), ("x", 1), ("z", 1, 3), ("xlast", 1), ("z", 1, 4),
+    ("pairlast", 1), ("rf", 2), ("pair", 2), ("pleft", 1), ("pright", 1), ("odd", 0), ("top", 0), ("top", 1),
+    ("odd", 1), ("odd", 2), ("z", 2, 1), ("line", 2), ("z", 2, 2), ("x", 2), ("z", 2, 3), ("xlast", 2), ("z", 2, 4),
+    ("pairlast", 2), ("pleft", 2), ("pright", 2), ("block2", 1, 0), ("returned", 0), ("block2", 0, 1),
+    ("returned", 1), ("block2", 0, 0), ("returned", 2), ("block2", 1, 1),
 )
 
 
@@ -441,9 +440,21 @@
                 give(kind, 2)
             unmoved()
 
-    def returned():
-        for key, cond in give_cond.items():
+    def returned(w):
+        def arrive(key, cond):
             pl.when(cond)(back[key].wait_recv)
+
+        for kind in ("12", "21", "22"):
+            key = kind, w
+            if w == 1 and kind != "21":
+                arrive(key, give_cond[key] & (c > 0))
+            else:
+                arrive(key, give_cond[key])
+            if w == 0 and kind != "21":
+                arrive((kind, 1), give_cond[kind, 1] & (c == 0))
+        if w == 0:
+            for l in range(2):
+                arrive(("h", l), give_cond["h", l])
 
     stores = []
 

time: 165 us -> 163 us (0.988); the launches traced: 165 us -> 160 us
  Pallas kernels: 160 us -> 155 us
    pallas_call x1, Pallas kernels: 160 us -> 155 us  [local(): pl.pallas_call(kernel, out_shape=jax.ShapeDtypeStruct(hessenberg.shape, F...]
where the time goes in v3:
time: 163 us; the launch traced here: 160 us
  Pallas kernels  155 us (95%)
  local copies, waits for them, and re-layouts  4.79 us (3%)
    pallas_call x1, Pallas kernels, local(): pl.pallas_call(kernel, out_shape=jax.ShapeDtypeStruct(hessenberg.shape, F...  155 us
    unnamed x1, local copies, waits for them, and re-layouts  4.79 us

profile of v3, /device:TPU:8, one launch (start us, length us, event | category | flops | bytes accessed | tf_op | source)
XLA Modules:
  0.0 159.9 jit_solution(4619975330674198309)
XLA Ops:
  0.0 155.1 %sweep.1 = f32[1024,1024]{1,0:T(8,128)} custom-call(s32[3,32]{1,0:T(4,128)} %flags.1, f32[1024,1024]{1,0:T(8,128)} %hess.1, f32[3,2,32,512]{3,2,1,0:T(8,128)} %fac.1), custom_call_target="tpu_custom_call" | custom-call | tf_op jit(solution)/shard_map/sweep/pallas_call | solution.py:489
  155.1 4.8 %copy.5 = f32[1024,1024]{1,0:T(8,128)} copy(f32[1024,1024]{1,0:T(8,128)} %sweep.1) | data formatting | bytes 8388608
